TPU v7x, 32 devices: a whole 2x2x4 slice. The times are simulated.
32 devices in a mesh: stn: 8 (over z, core), chan: 4 (over y, x).
Axes of the slice: x: 2, y: 2, z: 4, core: 2. Of those that a mesh axis runs over, the one named last changes fastest.
Arguments:
- voltages: bfloat16 [64, 32, 2, 1024], P('stn', 'chan'), may hold values from -6 to 6
- filter_taps: float32 [16, 1024], replicated, may hold values from -1.5 to 1.5
Outputs:
- visibilities: bfloat16 [1024, 2, 64, 64], P('chan', None, 'stn')
All inputs are finite; a program needn't handle non-finite values.
Results may differ from a plain program's by a relative error of at most 0.0069.
Values may be sent and summed in bfloat16 or wider, within the bound.
A program may use at most 64 MiB of HBM per device.

v0:
```python
import math

import jax
import jax.numpy as jnp
from jax import lax
from jax.sharding import PartitionSpec as P


def from_behind(array, axis, by):
    devices = lax.axis_size(axis)
    pairs = [(i, i + by) for i in range(devices) if 0 <= i + by < devices]
    return lax.ppermute(array, axis, pairs)


def passed_along(value, axis, steps):
    count = lax.axis_size(axis)
    pairs = [(source, (source + steps) % count) for source in range(count)]
    return lax.ppermute(value, axis, pairs)


def fourier_matrix(points):
    sample_index = jnp.arange(points, dtype=jnp.int32)
    phase = sample_index[:, None] * sample_index[None, :] % points
    angle = phase.astype(jnp.float32) * (2.0 * math.pi / points)
    norm_factor = 1.0 / math.sqrt(points)
    cosine = (jnp.cos(angle) * norm_factor).astype(jnp.bfloat16)
    sine_part = (-jnp.sin(angle) * norm_factor).astype(jnp.bfloat16)
    upper_rows = jnp.stack([cosine, sine_part], axis=2)
    lower_rows = jnp.stack([-sine_part, cosine], axis=2)
    return jnp.concatenate([upper_rows, lower_rows], axis=0).reshape(2 * points, 2 * points)


def history_frames(voltages, history_len):
    frames_here = voltages.shape[1]
    shift_count = (history_len - 1) // frames_here + 1
    earlier = []
    for distance in range(1, shift_count + 1):
        keep_count = min(frames_here, history_len - (distance - 1) * frames_here)
        received_frames = from_behind(voltages[:, frames_here - keep_count :], "chan", distance)
        earlier = [received_frames] + earlier
    return jnp.concatenate(earlier + [voltages], axis=1)


def correlate(local_block, swapped, other_block, factor):
    real_part = jnp.einsum(
        "kcas,kcbs->kab", local_block, other_block, preferred_element_type=jnp.float32
    )
    imag_part = jnp.einsum(
        "kcas,kcbs->kab", swapped, other_block, preferred_element_type=jnp.float32
    )
    return jnp.stack([real_part, imag_part], axis=1) * factor


def mirrored(product):
    return jnp.stack(
        [jnp.swapaxes(product[:, 0], 1, 2), -jnp.swapaxes(product[:, 1], 1, 2)], axis=1
    )


def place_block(buffer, product, chan_start, slot_index):
    columns = product.shape[3]
    anchor = jnp.int32(0)
    return lax.dynamic_update_slice(
        buffer, product, (jnp.int32(chan_start), anchor, anchor, slot_index * columns)
    )


def per_device(voltages, filter_taps):
    inputs_here, frames_here, parts, points = voltages.shape
    tap_count = filter_taps.shape[0]
    extended = history_frames(voltages, tap_count - 1)
    filtered = jnp.zeros(voltages.shape, jnp.float32)
    for tap_index in range(tap_count):
        offset = tap_count - 1 - tap_index
        filtered = filtered + filter_taps[tap_index][None, None, None, :] * extended[
            :, offset : offset + frames_here
        ].astype(jnp.float32)
    filtered = filtered.astype(jnp.bfloat16).reshape(inputs_here, frames_here, parts * points)
    matrix = fourier_matrix(points)
    spectra = jnp.einsum("isr,rq->qis", filtered, matrix, preferred_element_type=jnp.float32)
    spectra = spectra.reshape(points, parts, inputs_here, frames_here).astype(jnp.bfloat16)
    local_block = lax.all_to_all(spectra, "chan", split_axis=0, concat_axis=3, tiled=True)
    cycle_size = lax.axis_size("stn")
    position = lax.axis_index("stn")
    halfway = cycle_size // 2
    channels = local_block.shape[0]
    factor = 1.0 / local_block.shape[3]
    swapped = jnp.stack([local_block[:, 1], -local_block[:, 0]], axis=1)
    row_sums = jnp.zeros((channels, parts, inputs_here, cycle_size * inputs_here), jnp.float32)
    row_sums = place_block(
        row_sums, correlate(local_block, swapped, local_block, factor), 0, position
    )
    mirror = jnp.zeros(row_sums.shape, jnp.bfloat16)

    def cycle_turn(step_index, carry):
        moving_block, row_sums, mirror = carry
        moving_block = passed_along(moving_block, "stn", -1)
        slot_index = (position + step_index) % cycle_size
        is_kept = jnp.logical_or(step_index < halfway, position < halfway)
        product = jnp.where(is_kept, correlate(local_block, swapped, moving_block, factor), 0.0)
        row_sums = place_block(row_sums, product, 0, slot_index)
        outgoing = mirrored(product).astype(jnp.bfloat16)
        mirror = place_block(mirror, outgoing, 0, slot_index)
        return (moving_block, row_sums, mirror)

    moving_block, row_sums, mirror = lax.fori_loop(
        1, halfway + 1, cycle_turn, (local_block, row_sums, mirror)
    )
    returned = lax.all_to_all(mirror, "stn", split_axis=3, concat_axis=3, tiled=True)
    row_sums = row_sums + returned.astype(jnp.float32)
    return row_sums.astype(jnp.bfloat16)


def solution(mesh):
    placed = (P("stn", "chan", None, None), P())
    return jax.shard_map(
        per_device,
        mesh=mesh,
        in_specs=placed,
        out_specs=P("chan", None, "stn", None),
        check_vma=False,
    )
```

profile of v0, /device:TPU:0, one launch (start us, length us, event | category | flops | bytes accessed | tf_op | source)
XLA Modules:
  0.0 217.8 jit_solution(14949994201829251121)
XLA Ops:
  0.0 4.8 %collective-permute-start.1 = (bf16[8,8,2,1024]{3,2,1,0:T(2,128)(2,1)}, bf16[8,8,2,1024]{3,2,1,0:T(2,128)(2,1)S(1)}, u32[]{:S(2)}, u32[]{:S(2)}) collective-permute-start(bf16[8,8,2,1024]{3,2,1,0:T(2,128)(2,1)} %param.4), channel_id=1, source_target_pairs={{0,1},{1,2},{2,3},{4,5},{5,6},{6,7},{8,9},{9,10},{10,11},{12,13},{... | collective-permute-start | bytes 786440 | tf_op jit(solution)/shard_map/ppermute | solution.py:12
  9.4 17.1 %multiply_convert_fusion = (bf16[1024,1024,1]{1,0,2:T(8,128)(2,1)S(1)}, bf16[1024,1024,1]{1,0,2:T(8,128)(2,1)S(1)}) fusion(), kind=kLoop, calls=%fused_computation.21 | loop fusion | flops 19922944 | bytes 4194304 | tf_op jit(solution)/shard_map/convert_element_type | solution.py:27
  26.6 15.8 %fusion.16 = bf16[1024,1024,1]{1,0,2:T(8,128)(2,1)S(1)} fusion(), kind=kLoop, calls=%fused_computation.31 | loop fusion | flops 20971520 | bytes 2097152 | tf_op jit(solution)/shard_map/neg | solution.py:29
  42.4 4.0 %maximum_maximum_fusion = bf16[2048,1024,2]{1,0,2:T(8,128)(2,1)} fusion(bf16[1024,1024,1]{1,0,2:T(8,128)(2,1)S(1)} %get-tuple-element.262, bf16[1024,1024,1]{1,0,2:T(8,128)(2,1)S(1)} %fusion.16, bf16[1024,1024,1]{1,0,2:T(8,128)(2,1)S(1)} %get-tuple-element.261), kind=kLoop, calls=%fused_computation.12 | loop fusion | flops 33554432 | bytes 14680064 | tf_op jit(solution)/shard_map/concatenate | solution.py:30
  46.4 21.5 %copy.62 = bf16[2048,1024,2]{0,2,1:T(2,128)(2,1)} copy(bf16[2048,1024,2]{1,0,2:T(8,128)(2,1)} %maximum_maximum_fusion) | data formatting | bytes 16777216 | tf_op jit(solution)/shard_map/concatenate | solution.py:30
  67.9 13.1 %reshape.119 = bf16[2048,2048]{0,1:T(8,128)(2,1)} reshape(bf16[2048,1024,2]{0,2,1:T(2,128)(2,1)} %copy.62) | data formatting | bytes 16777216 | tf_op jit(solution)/shard_map/reshape | solution.py:30
  81.0 14.2 %dot_general.34 = bf16[1024,2,2048]{2,1,0:T(2,128)(2,1)} reshape(bf16[2048,2048]{1,0:T(8,128)(2,1)} %bitcast.78) | data formatting | bytes 16777216 | tf_op jit(solution)/shard_map/isr,rq->qis/dot_general | solution.py:80
  96.0 3.8 %add_convert_fusion = bf16[8,8,2,1024]{3,2,1,0:T(2,128)(2,1)S(1)} fusion(bf16[8,8,2,1024]{3,2,1,0:T(2,128)(2,1)S(1)} %collective-permute-done.1, bf16[8,8,2,1024]{3,2,1,0:T(2,128)(2,1)S(1)} %copy-done.1, bf16[8,15,2,1024]{3,2,1,0:T(2,128)(2,1)S(1)} %get-tuple-element.244, bf16[8,16,2,1024]{3,2,1,0:T(2,128)(2,1)S(1)} %constant_dynamic-update-slice_fusion.1, ...), kind=kLoop, calls=%fused_computation.32 | loop fusion | flops 6291456 | bytes 4521984 | tf_op jit(solution)/shard_map/convert_element_type | solution.py:78
  100.0 8.2 %fusion.12 = bf16[1024,2,8,8]{0,3,2,1:T(8,128)(2,1)S(1)} fusion(bf16[8,8,2048,1]{2,1,0,3:T(8,128)(2,1)S(1)} %reshape.124, bf16[1024,2,2048,1]{2,1,0,3:T(2,128)(2,1)} %bitcast.80), kind=kOutput, calls=%fused_computation.28 | convolution fusion | flops 537001984 | bytes 8912896 | tf_op jit(solution)/shard_map/isr,rq->qis/dot_general | solution.py:80
  108.3 4.7 %copy.64 = bf16[1024,2,8,8]{3,2,1,0:T(8,128)(2,1)} copy(bf16[1024,2,8,8]{0,3,2,1:T(8,128)(2,1)S(1)} %fusion.12) | data formatting | bytes 524288 | tf_op jit(solution)/shard_map/convert_element_type | solution.py:81
  113.0 6.4 %reshape.128 = bf16[4,2,16384]{2,1,0:T(2,128)(2,1)} reshape(bf16[1024,2,8,8]{3,2,1,0:T(8,128)(2,1)} %copy.64) | data formatting | bytes 524288
  119.4 3.4 %all-to-all-start = ((bf16[4,2,16384]{2,1,0:T(2,128)(2,1)}), bf16[4,2,16384]{2,1,0:T(2,128)(2,1)S(1)}, u32[]{:S(2)}, u32[]{:S(2)}) async-start(bf16[4,2,16384]{2,1,0:T(2,128)(2,1)} %reshape.128), calls=%async_computation | async-start | bytes 524288 | tf_op jit(solution)/shard_map/all_to_all | solution.py:82
  122.8 5.3 %all-to-all-done = bf16[4,2,16384]{2,1,0:T(2,128)(2,1)S(1)} async-done(((bf16[4,2,16384]{2,1,0:T(2,128)(2,1)}), bf16[4,2,16384]{2,1,0:T(2,128)(2,1)S(1)}, u32[]{:S(2)}, u32[]{:S(2)}) %all-to-all-start) | async-done | bytes 262176 | tf_op jit(solution)/shard_map/all_to_all | solution.py:82
  128.1 5.9 %reshape.129 = bf16[1024,2,8,8]{3,2,1,0:T(8,128)(2,1)} reshape(bf16[4,2,16384]{2,1,0:T(2,128)(2,1)S(1)} %all-to-all-done) | data formatting | bytes 524288
  134.1 4.7 %copy.85 = bf16[4,256,2,8,8]{1,0,4,3,2:T(4,128)(2,1)S(1)} copy(bf16[4,256,2,8,8]{4,3,2,1,0:T(8,128)(2,1)} %bitcast.79) | data formatting | bytes 524288 | tf_op jit(solution)/shard_map/all_to_all | solution.py:82
  145.8 48.9 %while.19 = (s32[]{:T(128)}, bf16[256,2,8,32]{0,3,2,1:T(8,128)(2,1)S(1)}, f32[256,2,8,64]{0,3,2,1:T(8,128)}, bf16[256,2,8,64]{0,2,1,3:T(8,128)(2,1)}, pred[]{:T(...) while((s32[]{:T(128)}, ...), condition=%wide.region_1.2_spmd, body=%wide.region_0.1_spmd.sunk | while | flops 4358164 | bytes 4489577 | solution.py:106
  147.1 3.9 %collective-permute-done = bf16[256,2,8,32]{0,3,2,1:T(8,128)(2,1)S(1)} collective-permute-done((bf16[256,2,8,32]{0,3,2,1:T(8,128)(2,1)S(1)}, bf16[256,2,8,32]{0,3,2,1:T(8,128)(2,1)S(1)}, u32[]{:S(2)}, u32[]{:S(2)}) %collective-permute-start) | collective-permute-done | bytes 262176 | tf_op jit(solution)/shard_map/while/body/eval_jaxpr/ppermute | solution.py:18
  156.2 3.8 %collective-permute-start = (bf16[256,2,8,32]{0,3,2,1:T(8,128)(2,1)S(1)}, bf16[256,2,8,32]{0,3,2,1:T(8,128)(2,1)S(1)}, u32[]{:S(2)}, u32[]{:S(2)}) collective-permute-start(bf16[256,2,8,32]{0,3,2,1:T(8,128)(2,1)S(1)} %get-tuple-element.331), channel_id=1, source_target_pairs={{0,28},{4,0},{8,4},{12,8},{16,12},{20,16},{24,20},{28,24},{1,29},{... | collective-permute-start | bytes 786440 | tf_op jit(solution)/shard_map/while/body/eval_jaxpr/ppermute | solution.py:18
  160.0 3.9 %collective-permute-done = bf16[256,2,8,32]{0,3,2,1:T(8,128)(2,1)S(1)} collective-permute-done((bf16[256,2,8,32]{0,3,2,1:T(8,128)(2,1)S(1)}, bf16[256,2,8,32]{0,3,2,1:T(8,128)(2,1)S(1)}, u32[]{:S(2)}, u32[]{:S(2)}) %collective-permute-start) | collective-permute-done | bytes 262176 | tf_op jit(solution)/shard_map/while/body/eval_jaxpr/ppermute | solution.py:18
  169.0 3.8 %collective-permute-start = (bf16[256,2,8,32]{0,3,2,1:T(8,128)(2,1)S(1)}, bf16[256,2,8,32]{0,3,2,1:T(8,128)(2,1)S(1)}, u32[]{:S(2)}, u32[]{:S(2)}) collective-permute-start(bf16[256,2,8,32]{0,3,2,1:T(8,128)(2,1)S(1)} %get-tuple-element.331), channel_id=1, source_target_pairs={{0,28},{4,0},{8,4},{12,8},{16,12},{20,16},{24,20},{28,24},{1,29},{... | collective-permute-start | bytes 786440 | tf_op jit(solution)/shard_map/while/body/eval_jaxpr/ppermute | solution.py:18
  172.8 3.9 %collective-permute-done = bf16[256,2,8,32]{0,3,2,1:T(8,128)(2,1)S(1)} collective-permute-done((bf16[256,2,8,32]{0,3,2,1:T(8,128)(2,1)S(1)}, bf16[256,2,8,32]{0,3,2,1:T(8,128)(2,1)S(1)}, u32[]{:S(2)}, u32[]{:S(2)}) %collective-permute-start) | collective-permute-done | bytes 262176 | tf_op jit(solution)/shard_map/while/body/eval_jaxpr/ppermute | solution.py:18
  181.9 3.7 %collective-permute-start = (bf16[256,2,8,32]{0,3,2,1:T(8,128)(2,1)S(1)}, bf16[256,2,8,32]{0,3,2,1:T(8,128)(2,1)S(1)}, u32[]{:S(2)}, u32[]{:S(2)}) collective-permute-start(bf16[256,2,8,32]{0,3,2,1:T(8,128)(2,1)S(1)} %get-tuple-element.331), channel_id=1, source_target_pairs={{0,28},{4,0},{8,4},{12,8},{16,12},{20,16},{24,20},{28,24},{1,29},{... | collective-permute-start | bytes 786440 | tf_op jit(solution)/shard_map/while/body/eval_jaxpr/ppermute | solution.py:18
  185.6 3.9 %collective-permute-done = bf16[256,2,8,32]{0,3,2,1:T(8,128)(2,1)S(1)} collective-permute-done((bf16[256,2,8,32]{0,3,2,1:T(8,128)(2,1)S(1)}, bf16[256,2,8,32]{0,3,2,1:T(8,128)(2,1)S(1)}, u32[]{:S(2)}, u32[]{:S(2)}) %collective-permute-start) | collective-permute-done | bytes 262176 | tf_op jit(solution)/shard_map/while/body/eval_jaxpr/ppermute | solution.py:18
  194.7 20.3 %all_to_all.23 = bf16[256,2,8,64]{0,2,1,3:T(8,128)(2,1)S(1)} all-to-all(bf16[256,2,8,64]{0,2,1,3:T(8,128)(2,1)} %get-tuple-element.190), channel_id=1, replica_groups=mesh['stn'=8,'chan'=4] {'stn'}, dimensions={3} | all-to-all | bytes 1048576 | tf_op jit(solution)/shard_map/all_to_all | solution.py:109
  (82 shorter events, 37.1 us)
Async XLA Ops:
  0.0 95.4 %collective-permute-start.1 = (bf16[8,8,2,1024]{3,2,1,0:T(2,128)(2,1)}, bf16[8,8,2,1024]{3,2,1,0:T(2,128)(2,1)S(1)}, u32[]{:S(2)}, u32[]{:S(2)}) collective-permute-start(bf16[8,8,2,1024]{3,2,1,0:T(2,128)(2,1)} %param.4), channel_id=1, source_target_pairs={{0,1},{1,2},{2,3},{4,5},{5,6},{6,7},{8,9},{9,10},{10,11},{12,13},{... | collective-permute-start | bytes 786440 | tf_op jit(solution)/shard_map/ppermute | solution.py:12
  6.0 89.2 %collective-permute-start.2 = (bf16[8,7,2,1024]{3,2,1,0:T(2,128)(2,1)S(1)}, bf16[8,7,2,1024]{3,2,1,0:T(2,128)(2,1)S(1)}, u32[]{:S(2)}, u32[]{:S(2)}) collective-permute-start(bf16[8,7,2,1024]{3,2,1,0:T(2,128)(2,1)S(1)} %slice.151), channel_id=1, source_target_pairs={{0,2},{1,3},{4,6},{5,7},{8,10},{9,11},{12,14},{13,15},{16,18},{17,... | collective-permute-start | bytes 688136 | tf_op jit(solution)/shard_map/ppermute | solution.py:12
  81.0 14.2 %copy-start.2 = (f32[16,1024]{1,0:T(8,128)S(1)}, f32[16,1024]{1,0:T(8,128)}, u32[]{:S(2)}) copy-start(f32[16,1024]{1,0:T(8,128)} %param.5) | copy-start | bytes 196612
  81.0 14.8 %copy-start.1 = (bf16[8,8,2,1024]{3,2,1,0:T(2,128)(2,1)S(1)}, bf16[8,8,2,1024]{3,2,1,0:T(2,128)(2,1)}, u32[]{:S(2)}) copy-start(bf16[8,8,2,1024]{3,2,1,0:T(2,128)(2,1)} %param.4) | copy-start | bytes 786436
  119.4 8.8 %all-to-all-start = ((bf16[4,2,16384]{2,1,0:T(2,128)(2,1)}), bf16[4,2,16384]{2,1,0:T(2,128)(2,1)S(1)}, u32[]{:S(2)}, u32[]{:S(2)}) async-start(bf16[4,2,16384]{2,1,0:T(2,128)(2,1)} %reshape.128), calls=%async_computation | async-start | bytes 524288 | tf_op jit(solution)/shard_map/all_to_all | solution.py:82
  144.6 1.2 copy-start
  145.8 5.2 %collective-permute-start = (bf16[256,2,8,32]{0,3,2,1:T(8,128)(2,1)S(1)}, bf16[256,2,8,32]{0,3,2,1:T(8,128)(2,1)S(1)}, u32[]{:S(2)}, u32[]{:S(2)}) collective-permute-start(bf16[256,2,8,32]{0,3,2,1:T(8,128)(2,1)S(1)} %get-tuple-element.331), channel_id=1, source_target_pairs={{0,28},{4,0},{8,4},{12,8},{16,12},{20,16},{24,20},{28,24},{1,29},{... | collective-permute-start | bytes 786440 | tf_op jit(solution)/shard_map/while/body/eval_jaxpr/ppermute | solution.py:18
  156.2 7.7 %collective-permute-start = (bf16[256,2,8,32]{0,3,2,1:T(8,128)(2,1)S(1)}, bf16[256,2,8,32]{0,3,2,1:T(8,128)(2,1)S(1)}, u32[]{:S(2)}, u32[]{:S(2)}) collective-permute-start(bf16[256,2,8,32]{0,3,2,1:T(8,128)(2,1)S(1)} %get-tuple-element.331), channel_id=1, source_target_pairs={{0,28},{4,0},{8,4},{12,8},{16,12},{20,16},{24,20},{28,24},{1,29},{... | collective-permute-start | bytes 786440 | tf_op jit(solution)/shard_map/while/body/eval_jaxpr/ppermute | solution.py:18
  169.0 7.7 %collective-permute-start = (bf16[256,2,8,32]{0,3,2,1:T(8,128)(2,1)S(1)}, bf16[256,2,8,32]{0,3,2,1:T(8,128)(2,1)S(1)}, u32[]{:S(2)}, u32[]{:S(2)}) collective-permute-start(bf16[256,2,8,32]{0,3,2,1:T(8,128)(2,1)S(1)} %get-tuple-element.331), channel_id=1, source_target_pairs={{0,28},{4,0},{8,4},{12,8},{16,12},{20,16},{24,20},{28,24},{1,29},{... | collective-permute-start | bytes 786440 | tf_op jit(solution)/shard_map/while/body/eval_jaxpr/ppermute | solution.py:18
  181.9 7.6 %collective-permute-start = (bf16[256,2,8,32]{0,3,2,1:T(8,128)(2,1)S(1)}, bf16[256,2,8,32]{0,3,2,1:T(8,128)(2,1)S(1)}, u32[]{:S(2)}, u32[]{:S(2)}) collective-permute-start(bf16[256,2,8,32]{0,3,2,1:T(8,128)(2,1)S(1)} %get-tuple-element.331), channel_id=1, source_target_pairs={{0,28},{4,0},{8,4},{12,8},{16,12},{20,16},{24,20},{28,24},{1,29},{... | collective-permute-start | bytes 786440 | tf_op jit(solution)/shard_map/while/body/eval_jaxpr/ppermute | solution.py:18
where the time goes:
time: 220 us; the launch traced here: 218 us
  local copies, waits for them, and re-layouts  87.8 us (40%)
  other arithmetic  45.6 us (21%)
  starting transfers between devices  24.3 us (11%)
  waiting for transfers between devices  20.9 us (10%)
  blocking collectives  20.3 us (9%)
  matrix products  18.5 us (8%)
    concatenate x1, local copies, waits for them, and re-layouts, fourier_matrix(): jnp.concatenate([upper_rows, lower_rows], axis=0)  21.5 us
    all_to_all x1, blocking collectives, per_device(): lax.all_to_all(mirror, 'stn', split_axis=3, concat_axis=3, tiled=True)  20.3 us
    convert_element_type x1, other arithmetic, fourier_matrix(): sine_part = (-jnp.sin(angle) * norm_factor).astype(jnp.bfloat16)  17.1 us
    neg x1, other arithmetic, fourier_matrix(): lower_rows = jnp.stack([-sine_part, cosine], axis=2)  15.8 us
    ppermute x4, waiting for transfers between devices, passed_along(): return lax.ppermute(value, axis, pairs)  15.6 us
    dot_general x1, local copies, waits for them, and re-layouts, per_device(): jnp.einsum('isr,rq->qis', filtered, matrix, preferred_element_type=jnp.fl...  14.2 us
    unnamed x10, local copies, waits for them, and re-layouts  13.2 us
    reshape x1, local copies, waits for them, and re-layouts, fourier_matrix(): jnp.concatenate([upper_rows, lower_rows], axis=0)  13.1 us
  transfers between devices with their start and end apart: 7, of which 5 were waited for; matrix products, arithmetic and copies ran while one was open for 40% of the time, Pallas kernels for 0%

commit v1 on v0

--- a/solution.py
+++ b/solution.py
@@ -1,9 +1,18 @@
+import functools
 import math
 
 import jax
 import jax.numpy as jnp
+import numpy as np
 from jax import lax
+from jax.experimental import pallas as pl
+from jax.experimental.pallas import tpu as pltpu
 from jax.sharding import PartitionSpec as P
+
+MESH = pl.DeviceIdType.MESH
+NT = (((1,), (1,)), ((), ()))
+LANES = 128
+SUB = 8
 
 
 def from_behind(array, axis, by):
@@ -111,10 +120,253 @@
     return row_sums.astype(jnp.bfloat16)
 
 
+def fourier_rows(points):
+    index = np.arange(points, dtype=np.int64)
+    angle = (index[:, None] * index[None, :] % points).astype(np.float64) * (2.0 * np.pi / points)
+    norm_factor = 1.0 / math.sqrt(points)
+    both = np.concatenate([np.cos(angle) * norm_factor, -np.sin(angle) * norm_factor], axis=1)
+    return both.astype(np.float32).astype(jnp.bfloat16)
+
+
+def fx_kernel(
+    n_stn, n_chan, frames, points, v_ref, taps_ref, four_hbm, out_ref,
+    four, xin, xf, rhs, spec, recv, rows_f, prod, gath,
+    four_sem, s1, r1, s2, r2, s3, r3,
+):
+    devices = n_stn * n_chan
+    p = lax.axis_index("stn")
+    q = lax.axis_index("chan")
+    me = p * n_chan + q
+    group = q * n_stn + p
+    chans = points // devices
+    tap_count = taps_ref.shape[0]
+    lane_tiles = points // LANES
+    n_four = four_sem.shape[0]
+    four_rows = points // n_four
+    n_part = s3.shape[0]
+    part_rows = chans // n_part
+
+    def four_copy(step):
+        chunk = lax.rem(group // (four_rows // chans) + step, n_four)
+        rows = pl.ds(pl.multiple_of(chunk * four_rows, four_rows), four_rows)
+        return chunk, pltpu.make_async_copy(four_hbm.at[rows], four.at[rows], four_sem.at[chunk])
+
+    for step in range(n_four):
+        four_copy(step)[1].start()
+
+    barrier = pltpu.get_barrier_semaphore()
+
+    def greet(step, carry):
+        other = lax.rem(me + step, devices)
+        pl.semaphore_signal(
+            barrier, inc=1, device_id=(other // n_chan, lax.rem(other, n_chan)), device_id_type=MESH
+        )
+        return carry
+
+    lax.fori_loop(1, devices, greet, 0)
+    pl.semaphore_wait(barrier, devices - 1)
+
+    def in_copy(to, source):
+        return pltpu.make_async_remote_copy(
+            src_ref=v_ref.at[to], dst_ref=xin.at[source], send_sem=s1.at[to], recv_sem=r1.at[source],
+            device_id=(p, to), device_id_type=MESH,
+        )
+
+    for step in range(1, n_chan):
+        in_copy(lax.rem(q + step, n_chan), q).start()
+
+    pad = xf.shape[2] - frames
+    per = frames // n_chan
+    xf[:, :, :pad, :] = jnp.zeros((xf.shape[0], xf.shape[1], pad, LANES), jnp.float32)
+
+    def widen(ref, source):
+        rows = pl.ds(pl.multiple_of(pad + source * per, per), per)
+        for tile in range(lane_tiles):
+            xf[:, tile, rows, :] = ref[:, :, tile * LANES : (tile + 1) * LANES].astype(jnp.float32)
+
+    widen(v_ref.at[q], q)
+    for step in range(1, n_chan):
+        source = lax.rem(q + step, n_chan)
+        in_copy(source, source).wait_recv()
+        widen(xin.at[source], source)
+
+    def fir(e, carry):
+        for c in range(2):
+            for tile in range(lane_tiles):
+                lanes = slice(tile * LANES, (tile + 1) * LANES)
+                total = jnp.zeros((frames, LANES), jnp.float32)
+                for tap in range(tap_count):
+                    total = total + taps_ref[tap : tap + 1, lanes] * xf[
+                        2 * e + c, tile, pad - tap : pad - tap + frames, :
+                    ]
+                here = pl.ds(pl.multiple_of((2 * e + c) * frames, frames), frames)
+                swap = pl.ds(pl.multiple_of((2 * e + 1 - c) * frames, frames), frames)
+                rhs[here, lanes] = total.astype(jnp.bfloat16)
+                other = slice(points + tile * LANES, points + (tile + 1) * LANES)
+                rhs[swap, other] = (total if c == 0 else -total).astype(jnp.bfloat16)
+        return carry
+
+    lax.fori_loop(0, xf.shape[0] // 2, fir, 0)
+
+    def spec_copy(to, source):
+        to_p, to_q = lax.rem(to, n_stn), to // n_stn
+        rows = pl.ds(pl.multiple_of(to * chans, chans), chans)
+        return pltpu.make_async_remote_copy(
+            src_ref=spec.at[rows], dst_ref=recv.at[source], send_sem=s2.at[to], recv_sem=r2.at[source],
+            device_id=(to_p, to_q), device_id_type=MESH,
+        )
+
+    for step in range(n_four):
+        chunk, copy = four_copy(step)
+        copy.wait()
+        rows = pl.ds(pl.multiple_of(chunk * four_rows, four_rows), four_rows)
+        spec[rows, :] = lax.dot_general(
+            four[rows, :], rhs[...], NT, preferred_element_type=jnp.float32
+        ).astype(jnp.bfloat16)
+        for sub in range(four_rows // chans):
+            to = chunk * (four_rows // chans) + sub
+
+            @pl.when(to != group)
+            def _():
+                spec_copy(to, me).start()
+
+    lane = lax.broadcasted_iota(jnp.int32, (chans, LANES), 1)
+    half, quarter = LANES // 2, LANES // 4
+
+    def spread(block, source):
+        wide = block.astype(jnp.float32)
+        by1, by2, by3 = (pltpu.roll(wide, quarter * n, 1) for n in (1, 2, 3))
+        first = jnp.where(lane < half, wide, jnp.where(lane < half + quarter, by1, -by3))
+        second = jnp.where(lane < half, by2, jnp.where(lane < half + quarter, by3, -by1))
+        rows_f[pl.ds(pl.multiple_of(2 * source * chans, chans), chans), :] = first
+        rows_f[pl.ds(pl.multiple_of((2 * source + 1) * chans, chans), chans), :] = second
+
+    spread(spec[pl.ds(pl.multiple_of(group * chans, chans), chans), :], me)
+
+    def take(step, carry):
+        source = lax.rem(me + step, devices)
+        spec_copy(source, source).wait_recv()
+        spread(recv[source], source)
+        return carry
+
+    lax.fori_loop(1, devices, take, 0)
+
+    def prod_copy(to, source, part):
+        rows = pl.ds(part * part_rows, part_rows)
+        return pltpu.make_async_remote_copy(
+            src_ref=prod.at[to, rows], dst_ref=gath.at[source, rows],
+            send_sem=s3.at[part, to], recv_sem=r3.at[part, source],
+            device_id=(to, q), device_id_type=MESH,
+        )
+
+    inputs = rows_f.shape[0] // chans
+    in_here = inputs // n_stn
+    left = lax.broadcasted_iota(jnp.int32, (inputs, LANES), 1) < half
+    for part in range(n_part):
+        for k in range(part * part_rows, (part + 1) * part_rows):
+            lhs = rows_f[pl.ds(k, inputs, stride=chans), :]
+            low = jnp.where(left, lhs, 0.0)
+            both = jnp.concatenate([low, pltpu.roll(low, half, 1)], axis=0).astype(jnp.bfloat16)
+            result = lax.dot_general(
+                lhs.astype(jnp.bfloat16), both, NT, preferred_element_type=jnp.float32
+            ) * (1.0 / frames)
+            prod[:, k] = result.reshape(n_stn, in_here, LANES).astype(jnp.bfloat16)
+        for step in range(1, n_stn):
+            prod_copy(lax.rem(p + step, n_stn), p, part).start()
+
+    def place(ref, source, part):
+        rows = slice(part * part_rows, (part + 1) * part_rows)
+        to = pl.ds(source * chans + part * part_rows, part_rows)
+        block = ref[rows]
+        out_ref[to, 0] = block[:, :, :half]
+        out_ref[to, 1] = block[:, :, half:]
+
+    for part in range(n_part):
+        place(prod.at[p], p, part)
+        for step in range(1, n_stn):
+            source = lax.rem(p + step, n_stn)
+            prod_copy(source, source, part).wait_recv()
+            place(gath.at[source], source, part)
+
+    for step in range(1, n_chan):
+        in_copy(lax.rem(q + step, n_chan), q).wait_send()
+
+    def sent(step, carry):
+        spec_copy(lax.rem(group + step, devices), me).wait_send()
+        return carry
+
+    lax.fori_loop(1, devices, sent, 0)
+    for part in range(n_part):
+        for step in range(1, n_stn):
+            prod_copy(lax.rem(p + step, n_stn), p, part).wait_send()
+
+
+def fused_device(n_stn, n_chan, voltages, filter_taps):
+    inputs_here, frames_here, parts, points = voltages.shape
+    devices = n_stn * n_chan
+    frames = frames_here * n_chan
+    inputs = inputs_here * n_stn
+    each = inputs_here // n_chan
+    chans = points // devices
+    n_four, n_part = 8, 4
+    split = voltages.reshape(n_chan, each, frames_here, parts, points)
+    split = split.transpose(0, 1, 3, 2, 4).reshape(n_chan, each * parts, frames_here, points)
+    matrix = jnp.asarray(fourier_rows(points))
+    vmem = pl.BlockSpec(memory_space=pltpu.VMEM)
+    return pl.pallas_call(
+        functools.partial(fx_kernel, n_stn, n_chan, frames, points),
+        out_shape=jax.ShapeDtypeStruct((points // n_chan, parts, inputs_here, inputs), jnp.bfloat16),
+        in_specs=[vmem, vmem, pl.BlockSpec(memory_space=pl.ANY)],
+        out_specs=vmem,
+        scratch_shapes=[
+            pltpu.VMEM((points, parts * points), jnp.bfloat16),
+            pltpu.VMEM((n_chan, each * parts, frames_here, points), jnp.bfloat16),
+            pltpu.VMEM((each * parts, points // LANES, frames + 16, LANES), jnp.float32),
+            pltpu.VMEM((each * parts * frames, parts * points), jnp.bfloat16),
+            pltpu.VMEM((points, LANES), jnp.bfloat16),
+            pltpu.VMEM((devices, chans, LANES), jnp.bfloat16),
+            pltpu.VMEM((inputs * chans, LANES), jnp.float32),
+            pltpu.VMEM((n_stn, chans, inputs_here, LANES), jnp.bfloat16),
+            pltpu.VMEM((n_stn, chans, inputs_here, LANES), jnp.bfloat16),
+            pltpu.SemaphoreType.DMA((n_four,)),
+            pltpu.SemaphoreType.DMA((n_chan,)),
+            pltpu.SemaphoreType.DMA((n_chan,)),
+            pltpu.SemaphoreType.DMA((devices,)),
+            pltpu.SemaphoreType.DMA((devices,)),
+            pltpu.SemaphoreType.DMA((n_part, n_stn)),
+            pltpu.SemaphoreType.DMA((n_part, n_stn)),
+        ],
+        compiler_params=pltpu.CompilerParams(
+            collective_id=0, has_side_effects=True, vmem_limit_bytes=48 * 1024 * 1024
+        ),
+    )(split, filter_taps, matrix)
+
+
+def fits(n_stn, n_chan, voltages, filter_taps):
+    inputs_here, frames_here, parts, points = voltages.shape
+    devices = n_stn * n_chan
+    return (
+        inputs_here == SUB
+        and frames_here == SUB
+        and parts == 2
+        and filter_taps.shape[0] <= 16
+        and n_chan * 2 == inputs_here
+        and 4 * n_chan * frames_here == LANES
+        and inputs_here * n_stn * 2 == LANES
+        and points % (devices * 32) == 0
+    )
+
+
+def on_device(n_stn, n_chan, voltages, filter_taps):
+    if fits(n_stn, n_chan, voltages, filter_taps):
+        return fused_device(n_stn, n_chan, voltages, filter_taps)
+    return per_device(voltages, filter_taps)
+
+
 def solution(mesh):
     placed = (P("stn", "chan", None, None), P())
     return jax.shard_map(
-        per_device,
+        functools.partial(on_device, mesh.shape["stn"], mesh.shape["chan"]),
         mesh=mesh,
         in_specs=placed,
         out_specs=P("chan", None, "stn", None),

time: 220 us -> 43.2 us (0.20)
  local copies, waits for them, and re-layouts: 87.8 us -> 5.67 us
  other arithmetic: 45.6 us -> 0 us
  Pallas kernels: 0 us -> 37.3 us
  starting transfers between devices: 24.3 us -> 0 us
  waiting for transfers between devices: 20.9 us -> 0 us
  blocking collectives: 20.3 us -> 0 us
  matrix products: 18.5 us -> 0 us
    pallas_call x0 -> x1, Pallas kernels: none -> 37.3 us  [fused_device(): pl.pallas_call(functools.partial(fx_kernel, n_stn, n_chan, frames, points...]
    convert_element_type x3 -> x0, other arithmetic: 22.7 us -> none  [the longest x1 17.1 us: fourier_matrix(): sine_part = (-jnp.sin(angle) * norm_factor).astype(jnp.bfloat16)]
    concatenate x2 -> x0, local copies, waits for them, and re-layouts: 21.7 us -> none  [the longest x1 21.5 us: fourier_matrix(): jnp.concatenate([upper_rows, lower_rows], axis=0)]
    ppermute x6 -> x0, starting transfers between devices: 20.9 us -> none  [the longest x4 12.6 us: passed_along(): return lax.ppermute(value, axis, pairs)]
    all_to_all x1 -> x0, blocking collectives: 20.3 us -> none  [per_device(): lax.all_to_all(mirror, 'stn', split_axis=3, concat_axis=3, tiled=True)]
    dot_general x11 -> x0, matrix products: 18.5 us -> none  [the longest x1 8.24 us: per_device(): jnp.einsum('isr,rq->qis', filtered, matrix, preferred_element_type=jnp.fl...]
    neg x1 -> x0, other arithmetic: 15.8 us -> none  [fourier_matrix(): lower_rows = jnp.stack([-sine_part, cosine], axis=2)]
    ppermute x6 -> x0, waiting for transfers between devices: 15.6 us -> none  [the longest x4 15.6 us: passed_along(): return lax.ppermute(value, axis, pairs)]
  transfers between devices with their start and end apart: 7 -> 0, of which waited for: 5 -> 0; matrix products, arithmetic and copies ran while one was open for 40% -> 0% of each run, Pallas kernels for 0% -> 0%
where the time goes in v1:
time: 43.2 us; the launch traced here: 43 us
  Pallas kernels  37.3 us (86%)
  local copies, waits for them, and re-layouts  5.67 us (13%)
    pallas_call x1, Pallas kernels, fused_device(): pl.pallas_call(functools.partial(fx_kernel, n_stn, n_chan, frames, points...  37.3 us
    unnamed x4, local copies, waits for them, and re-layouts  3.02 us
    pallas_call x1, local copies, waits for them, and re-layouts, fused_device(): pl.pallas_call(functools.partial(fx_kernel, n_stn, n_chan, frames, points...  1.65 us
    reshape x1, local copies, waits for them, and re-layouts, fused_device(): split = voltages.reshape(n_chan, each, frames_here, parts, points)  1 us

profile of v1, /device:TPU:0, one launch (start us, length us, event | category | flops | bytes accessed | tf_op | source)
XLA Modules:
  0.0 43.0 jit_solution(13690182031717932704)
XLA Ops:
  0.0 1.0 %copy.4 = bf16[4,2,8,2,1024]{4,2,3,1,0:T(8,128)(2,1)S(1)} copy(bf16[4,2,8,2,1024]{4,3,2,1,0:T(2,128)(2,1)} %bitcast.5) | data formatting | bytes 524288 | tf_op jit(solution)/shard_map/reshape | solution.py:312
  1.0 0.0 copy-start
  1.0 2.2 %copy-done = bf16[1024,2048]{1,0:T(8,128)(2,1)S(1)} copy-done((bf16[1024,2048]{1,0:T(8,128)(2,1)S(1)}, bf16[1024,2048]{1,0:T(8,128)(2,1)}, u32[]{:S(2)}) %copy-start) | copy-done | bytes 4194328
  3.2 0.0 copy-start.1
  3.2 0.8 %copy-done.1 = f32[16,1024]{1,0:T(8,128)S(1)} copy-done((f32[16,1024]{1,0:T(8,128)S(1)}, f32[16,1024]{1,0:T(8,128)}, u32[]{:S(2)}) %copy-start.1) | copy-done | bytes 65560
  4.0 37.3 %shard_map.37 = bf16[256,2,8,64]{3,2,1,0:T(8,128)(2,1)S(1)} custom-call(bf16[4,4,8,1024]{3,2,1,0:T(8,128)(2,1)S(1)} %bitcast.4, f32[16,1024]{1,0:T(8,128)S(1)} %copy-done.1, bf16[1024,2048]{1,0:T(8,128)(2,1)S(1)} %copy-done), custom_call_target="tpu_custom_call" | custom-call | tf_op jit(solution)/shard_map/pallas_call | solution.py:316
  41.4 1.6 %copy.5 = bf16[256,2,8,64]{0,3,2,1:T(8,128)(2,1)} copy(bf16[256,2,8,64]{3,2,1,0:T(8,128)(2,1)S(1)} %shard_map.37) | data formatting | bytes 1048576 | tf_op jit(solution)/shard_map/pallas_call | solution.py:316
Async XLA Ops:
  1.0 2.2 %copy-start = (bf16[1024,2048]{1,0:T(8,128)(2,1)S(1)}, bf16[1024,2048]{1,0:T(8,128)(2,1)}, u32[]{:S(2)}) copy-start(bf16[1024,2048]{1,0:T(8,128)(2,1)} %constant.2.clone.four_hbm) | copy-start | bytes 12582916
  3.2 0.8 %copy-start.1 = (f32[16,1024]{1,0:T(8,128)S(1)}, f32[16,1024]{1,0:T(8,128)}, u32[]{:S(2)}) copy-start(f32[16,1024]{1,0:T(8,128)} %taps_ref.1) | copy-start | bytes 196612
